TPU v7x, 128 devices: a whole 4x4x4 slice. The times are simulated.
128 devices in a mesh: tm: 64 (over z_hi, x, y, core), inp: 2 (over z_lo).
Axes of the slice: x: 4, y: 4, z: 4 (z_hi: 2, z_lo: 2; z = z_hi * 2 + z_lo), core: 2. Of those that a mesh axis runs over, the one named last changes fastest.
Arguments:
- voltages: bfloat16 [2, 262144, 1024], P(None, 'tm', 'inp'), may hold values from -127 to 127, as said below
- taps: int32 [12, 1024], replicated, may hold values from -64 to 64
Outputs:
- visibility: bfloat16 [512, 1024, 1024], P(('tm', 'inp'))
Inputs may be any that keep to these rules, and one draw needn't show every extreme that they name: `voltages`: every sample is a whole number.
All inputs are finite; a program needn't handle non-finite values.
Results may differ from a plain program's by a relative error of at most 0.0048.
Values may be sent and summed in bfloat16 or wider, within the bound.
A program may use at most 576 MiB of HBM per device.

v0:
```python
import math
import jax
import jax.numpy as jnp
from jax import lax
from jax.sharding import PartitionSpec as P

KEEP = 512


def passed_along(value, axis, steps):
    count = lax.axis_size(axis)
    first, last = (max(0, -steps), min(count, count - steps))
    return lax.ppermute(value, axis, [(source, source + steps) for source in range(first, last)])


def dft_table(fine_count, keep_count):
    branch = jnp.arange(fine_count, dtype=jnp.int32)[:, None]
    channel = jnp.arange(keep_count, dtype=jnp.int32)[None, :] - keep_count // 2
    phase_index = jnp.mod(branch * channel, fine_count).astype(jnp.float32)
    angles = 2.0 * math.pi / fine_count * phase_index
    norm_scale = 1.0 / math.sqrt(fine_count)
    cosine = jnp.cos(angles) * norm_scale
    sine_part = jnp.sin(angles) * norm_scale
    dft_matrix = jnp.stack(
        [jnp.stack([cosine, -sine_part], 1), jnp.stack([sine_part, cosine], 1)], 0
    )
    return dft_matrix.astype(jnp.bfloat16)


def finish(products, chan_count, all_inputs, spec_total):
    visibility = products.reshape(chan_count, 2, all_inputs, all_inputs) * (1.0 / spec_total)
    upper_mask = jnp.arange(all_inputs)[:, None] <= jnp.arange(all_inputs)[None, :]
    return jnp.where(upper_mask[None], visibility[:, 0], visibility[:, 1]).astype(jnp.bfloat16)


def per_device(voltages, taps):
    history_len = taps.shape[0] - 1
    fine_count = taps.shape[1]
    frames = voltages.shape[1] // fine_count
    input_width = voltages.shape[2]
    keep_count = KEEP
    coefficient = taps.astype(jnp.float32)
    dft_matrix = dft_table(fine_count, keep_count)
    n_time = lax.axis_size("tm")
    n_group = lax.axis_size("inp")
    chan_count = keep_count // (n_time * n_group)
    all_inputs = n_group * input_width
    spec_total = n_time * frames
    own_frames = voltages.reshape(2, frames, fine_count, input_width)
    pieces = [own_frames]
    remaining = history_len
    shift_count = (history_len + frames - 1) // frames
    for offset in range(1, shift_count + 1):
        take_count = min(remaining, frames)
        received = passed_along(own_frames[:, frames - take_count :], "tm", offset)
        pieces.insert(0, received)
        remaining = remaining - take_count
    extended = jnp.concatenate(pieces, axis=1)
    filtered = coefficient[0][None, None, :, None] * extended[
        :, history_len : history_len + frames
    ].astype(jnp.float32)
    for k in range(1, history_len + 1):
        filtered = filtered + coefficient[k][None, None, :, None] * extended[
            :, history_len - k : history_len - k + frames
        ].astype(jnp.float32)
    filtered = (filtered * (1.0 / 8192.0)).astype(jnp.bfloat16)
    spectra = jnp.einsum(
        "rfna,rnsj->jsfa", filtered, dft_matrix, preferred_element_type=jnp.float32
    ).astype(jnp.bfloat16)
    flat_spectra = spectra.reshape(keep_count, 2, frames * input_width)
    exchanged = lax.all_to_all(flat_spectra, ("tm", "inp"), split_axis=0, concat_axis=2, tiled=True)
    channel_grid = exchanged.reshape(chan_count, 2, n_time, n_group, frames, input_width)
    einsum_form = "crtgfa,csrthfb->csgahb"
    rotated = jnp.stack([-channel_grid[:, 1], channel_grid[:, 0]], axis=1)
    turned = jnp.stack([channel_grid, rotated], axis=1)
    products = jnp.einsum(einsum_form, channel_grid, turned, preferred_element_type=jnp.float32)
    return finish(products, chan_count, all_inputs, spec_total)


def solution(mesh):
    placed = (P(None, "tm", "inp"), P())
    return jax.shard_map(
        per_device,
        mesh=mesh,
        in_specs=placed,
        out_specs=P(("tm", "inp"), None, None),
        check_vma=False,
    )
```

profile of v0, /device:TPU:1, one launch (start us, length us, event | category | flops | bytes accessed | tf_op | source)
XLA Modules:
  0.0 758.6 jit_solution(5823844590932739800)
XLA Ops:
  0.0 11.4 %copy.11 = bf16[2,4,1024,512]{2,3,0,1:T(8,128)(2,1)} copy(bf16[2,4,1024,512]{3,2,1,0:T(8,128)(2,1)} %bitcast.81) | data formatting | bytes 16777216 | tf_op jit(solution)/shard_map/reshape | solution.py:49
  11.4 0.0 copy-start.3
  11.4 4.7 collective-permute-start.1
  16.0 3.5 collective-permute-start
  19.6 6.8 slice.130
  26.4 5.9 collective-permute-start.2
  32.3 0.0 copy-done.3
  32.3 8.8 %negate_convert_fusion = (bf16[1024,1,512]{2,0,1:T(8,128)(2,1)S(1)}, bf16[1024,1,512]{2,0,1:T(8,128)(2,1)S(1)}, bf16[1024,1,512]{2,0,1:T(8,128)(2,1)S(1)}) fusion(s32[512]{0:T(512)S(1)} %iota_add_fusion), kind=kLoop, calls=%fused_computation.35 | loop fusion | flops 10485760 | bytes 3147776 | tf_op jit(solution)/shard_map/convert.7
  41.1 1.8 maximum_bitcast_fusion.7
  42.9 377.9 %collective-permute-done.2 = bf16[2,3,1024,512]{2,3,0,1:T(8,128)(2,1)} collective-permute-done((bf16[2,3,1024,512]{2,3,0,1:T(8,128)(2,1)}, bf16[2,3,1024,512]{2,3,0,1:T(8,128)(2,1)}, u32[]{:S(2)}, u32[]{:S(2)}) %collective-permute-start.2) | collective-permute-done | bytes 6291488 | tf_op jit(solution)/shard_map/ppermute | solution.py:13
  420.8 6.8 constant_dynamic-update-slice_fusion.3
  427.6 0.0 collective-permute-done.1
  427.6 0.0 copy-start.1
  427.6 7.4 constant_dynamic-update-slice_fusion.1
  435.1 0.9 copy-done.1
  436.0 0.0 collective-permute-done
  436.0 0.0 copy-start.2
  436.0 3.3 copy-done.2
  439.3 7.6 %constant_dynamic-update-slice_fusion = bf16[2,8,1024,512]{2,3,0,1:T(8,128)(2,1)} fusion(bf16[2,8,1024,512]{2,3,0,1:T(8,128)(2,1)} %get-tuple-element.5, bf16[2,4,1024,512]{2,3,0,1:T(8,128)(2,1)} %copy-done.2), kind=kLoop, calls=%fused_computation.42 | loop fusion | bytes 16777216 | tf_op jit(solution)/shard_map/concatenate | solution.py:58
  446.9 38.9 %bitcast_convert_fusion = bf16[2,512,4,512]{1,3,2,0:T(8,128)(2,1)} fusion(bf16[2,7,1024,512]{2,3,0,1:T(8,128)(2,1)} %get-tuple-element.6, f32[1024]{0:T(1024)S(1)} %bitcast.84, f32[1024]{0:T(1024)S(1)} %bitcast.85, f32[1024]{0:T(1024)S(1)} %bitcast.86, bf16[2,4,1024,512]{2,3,0,1:T(8,128)(2,1)} %copy-done.1, f32[1024]{0:T(1024)S(1)} %bitcast.87, ...), kind=kOutput, calls=%fused_computation.17 | convolution fusion | flops 8793358336 | bytes 83935232 | tf_op jit(solution)/shard_map/rfna,rnsj->jsfa/dot_general | solution.py:67
  485.8 11.3 %copy.16 = bf16[512,2,2048]{2,1,0:T(2,128)(2,1)} copy(bf16[512,2,2048]{0,2,1:T(8,128)(2,1)} %bitcast.82) | data formatting | bytes 8388608 | tf_op jit(solution)/shard_map/reshape | solution.py:70
  497.1 80.0 %all-to-all-start = ((bf16[512,2,2048]{2,1,0:T(2,128)(2,1)}), bf16[512,2,2048]{2,1,0:T(2,128)(2,1)}, u32[]{:S(2)}, u32[]{:S(2)}) async-start(bf16[512,2,2048]{2,1,0:T(2,128)(2,1)} %copy.16), calls=%async_computation | async-start | bytes 8388608 | tf_op jit(solution)/shard_map/all_to_all | solution.py:71
  577.0 0.3 iota_compare_fusion
  577.3 53.5 %all-to-all-done = bf16[512,2,2048]{2,1,0:T(2,128)(2,1)} async-done(((bf16[512,2,2048]{2,1,0:T(2,128)(2,1)}), bf16[512,2,2048]{2,1,0:T(2,128)(2,1)}, u32[]{:S(2)}, u32[]{:S(2)}) %all-to-all-start) | async-done | bytes 4194336 | tf_op jit(solution)/shard_map/all_to_all | solution.py:71
  630.8 7.6 reshape.176
  638.4 7.6 %reshape.175 = bf16[4,1,2,64,2,4,512]{6,5,2,0,4,3,1:T(4,128)(2,1)} reshape(bf16[4,2,128,2048]{3,1,0,2:T(2,128)(2,1)} %bitcast.24) | data formatting | bytes 8388608 | tf_op jit(solution)/shard_map/stack;reshape | solution.py:75
  646.0 0.0 copy-start
  646.0 3.7 fusion.24
  649.8 1.2 copy.39
  650.9 2.4 copy_negate_fusion
  653.4 0.0 copy-done
  653.4 4.4 copy.21
  657.7 2.3 maximum_bitcast_fusion.4
  660.1 20.4 %fusion = bf16[4,2,2,512,2,512]{3,5,2,4,1,0:T(8,128)(2,1)} fusion(bf16[4,1,2,64,2,4,512]{6,3,2,5,4,1,0:T(8,128)(2,1)} %maximum_bitcast_fusion.4, bf16[4,1,2,64,2,4,512]{6,3,2,5,4,1,0:T(8,128)(2,1)} %copy.21, bf16[4,2,64,2,4,512,1,1]{5,4,1,0,3,2,7,6:T(4,128)(2,1)} %bitcast.80), kind=kOutput, calls=%fused_computation.1 | convolution fusion | flops 8623489024 | bytes 29360128 | tf_op jit(solution)/shard_map/crtgfa,csrthfb->csgahb/dot_general | solution.py:76
  680.5 41.5 %copy.23 = bf16[4,2,2,512,2,512]{5,4,3,2,1,0:T(2,128)(2,1)} copy(bf16[4,2,2,512,2,512]{3,5,2,4,1,0:T(8,128)(2,1)} %fusion) | data formatting | bytes 33554432 | tf_op jit(solution)/shard_map/mul | solution.py:31
  722.0 27.3 %mul.287 = bf16[4,2,1024,1024]{3,2,1,0:T(8,128)(2,1)} reshape(bf16[4,2,2,512,2,512]{5,4,3,2,1,0:T(2,128)(2,1)} %copy.23) | data formatting | bytes 33554432 | tf_op jit(solution)/shard_map/mul | solution.py:31
  749.3 9.3 %fusion.2 = bf16[4,1024,1024]{2,1,0:T(8,128)(2,1)} fusion(bf16[4,2,1024,1024]{3,2,1,0:T(8,128)(2,1)} %mul.287, pred[1024,1024]{1,0:T(8,128)(4,1)S(1)} %iota_compare_fusion), kind=kLoop, calls=%fused_computation.8 | loop fusion | flops 4194304 | bytes 26214400 | tf_op jit(solution)/shard_map/convert_element_type | solution.py:33
  (3 shorter events, 0.0 us)
Async XLA Ops:
  11.4 20.9 %copy-start.3 = (s32[12,1024]{1,0:T(8,128)S(1)}, s32[12,1024]{1,0:T(8,128)}, u32[]{:S(2)}) copy-start(s32[12,1024]{1,0:T(8,128)} %param.3) | copy-start | bytes 147460
  11.4 416.3 %collective-permute-start.1 = (bf16[2,4,1024,512]{2,3,0,1:T(8,128)(2,1)}, bf16[2,4,1024,512]{2,3,0,1:T(8,128)(2,1)S(1)}, u32[]{:S(2)}, u32[]{:S(2)}) collective-permute-start(bf16[2,4,1024,512]{2,3,0,1:T(8,128)(2,1)} %copy.11), channel_id=1, source_target_pairs={{0,4},{2,6},{4,8},{6,10},{8,12},{10,14},{12,16},{14,18},{16,20},{1... | collective-permute-start | bytes 25165832 | tf_op jit(solution)/shard_map/ppermute | solution.py:13
  16.0 420.0 %collective-permute-start = (bf16[2,4,1024,512]{2,3,0,1:T(8,128)(2,1)}, bf16[2,4,1024,512]{2,3,0,1:T(8,128)(2,1)S(1)}, u32[]{:S(2)}, u32[]{:S(2)}) collective-permute-start(bf16[2,4,1024,512]{2,3,0,1:T(8,128)(2,1)} %copy.11), channel_id=1, source_target_pairs={{0,2},{2,4},{4,6},{6,8},{8,10},{10,12},{12,14},{14,16},{16,18},{18... | collective-permute-start | bytes 25165832 | tf_op jit(solution)/shard_map/ppermute | solution.py:13
  26.4 394.4 %collective-permute-start.2 = (bf16[2,3,1024,512]{2,3,0,1:T(8,128)(2,1)}, bf16[2,3,1024,512]{2,3,0,1:T(8,128)(2,1)}, u32[]{:S(2)}, u32[]{:S(2)}) collective-permute-start(bf16[2,3,1024,512]{2,3,0,1:T(8,128)(2,1)} %slice.130), channel_id=1, source_target_pairs={{0,6},{2,8},{4,10},{6,12},{8,14},{10,16},{12,18},{14,20},{16,22},{... | collective-permute-start | bytes 18874376 | tf_op jit(solution)/shard_map/ppermute | solution.py:13
  427.6 8.3 %copy-start.1 = (bf16[2,4,1024,512]{2,3,0,1:T(8,128)(2,1)}, bf16[2,4,1024,512]{2,3,0,1:T(8,128)(2,1)S(1)}, u32[]{:S(2)}) copy-start(bf16[2,4,1024,512]{2,3,0,1:T(8,128)(2,1)S(1)} %collective-permute-done.1) | copy-start | bytes 25165828
  436.0 3.3 copy-start.2
  497.1 133.7 %all-to-all-start = ((bf16[512,2,2048]{2,1,0:T(2,128)(2,1)}), bf16[512,2,2048]{2,1,0:T(2,128)(2,1)}, u32[]{:S(2)}, u32[]{:S(2)}) async-start(bf16[512,2,2048]{2,1,0:T(2,128)(2,1)} %copy.16), calls=%async_computation | async-start | bytes 8388608 | tf_op jit(solution)/shard_map/all_to_all | solution.py:71
  646.0 7.4 copy-start
where the time goes:
time: 762 us; the launch traced here: 759 us
  waiting for transfers between devices  431 us (57%)
  local copies, waits for them, and re-layouts  149 us (20%)
  starting transfers between devices  94 us (12%)
  matrix products  59.3 us (8%)
  other arithmetic  24.9 us (3%)
    ppermute x3, waiting for transfers between devices, passed_along(): lax.ppermute(value, axis, [(source, source + steps) for source in range(f...  378 us
    all_to_all x1, starting transfers between devices, per_device(): lax.all_to_all(flat_spectra, ('tm', 'inp'), split_axis=0, concat_axis=2,...  80 us
    mul x2, local copies, waits for them, and re-layouts, finish(): products.reshape(chan_count, 2, all_inputs, all_inputs) * (1.0 / spec_total)  68.8 us
    all_to_all x1, waiting for transfers between devices, per_device(): lax.all_to_all(flat_spectra, ('tm', 'inp'), split_axis=0, concat_axis=2,...  53.5 us
    dot_general x1, matrix products, per_device(): jnp.einsum('rfna,rnsj->jsfa', filtered, dft_matrix, preferred_element_typ...  38.9 us
    dot_general x1, matrix products, per_device(): jnp.einsum(einsum_form, channel_grid, turned, preferred_element_type=jnp....  20.4 us
    unnamed x11, local copies, waits for them, and re-layouts  19.7 us
  transfers between devices with their start and end apart: 4, of which 2 were waited for; matrix products, arithmetic and copies ran while one was open for 4% of the time, Pallas kernels for 0%

commit v1 on v0

--- a/solution.py
+++ b/solution.py
@@ -68,7 +68,15 @@
         "rfna,rnsj->jsfa", filtered, dft_matrix, preferred_element_type=jnp.float32
     ).astype(jnp.bfloat16)
     flat_spectra = spectra.reshape(keep_count, 2, frames * input_width)
-    exchanged = lax.all_to_all(flat_spectra, ("tm", "inp"), split_axis=0, concat_axis=2, tiled=True)
+    exchanged = jnp.concatenate(
+        lax.all_to_all(
+            jnp.stack(jnp.split(flat_spectra, lax.axis_size(("tm", "inp")), axis=0)),
+            ("tm", "inp"),
+            0,
+            0,
+        ),
+        axis=2,
+    )
     channel_grid = exchanged.reshape(chan_count, 2, n_time, n_group, frames, input_width)
     einsum_form = "crtgfa,csrthfb->csgahb"
     rotated = jnp.stack([-channel_grid[:, 1], channel_grid[:, 0]], axis=1)

time: 762 us -> 1050 us (1.38); the launches traced: 759 us -> 1030 us
  local copies, waits for them, and re-layouts: 149 us -> 403 us
  other arithmetic: 24.9 us -> 61.1 us
  matrix products: 59.3 us -> 32.4 us
    another operation x0 -> x130, local copies, waits for them, and re-layouts: none -> 117 us  [the longest x129 109 us: per_device(): jnp.stack(jnp.split(flat_spectra, lax.axis_size(('tm', 'inp')), axis=0))]
    unnamed x11 -> x255, local copies, waits for them, and re-layouts: 19.7 us -> 107 us
    split x0 -> x135, local copies, waits for them, and re-layouts: none -> 75.7 us  [per_device(): jnp.split(flat_spectra, lax.axis_size(('tm', 'inp')), axis=0)]
    dot_general x0 -> x1, other arithmetic: none -> 37.1 us  [per_device(): jnp.einsum('rfna,rnsj->jsfa', filtered, dft_matrix, preferred_element_typ...]
    dot_general x1, matrix products: 38.9 us -> 11.7 us  [per_device(): jnp.einsum('rfna,rnsj->jsfa', filtered, dft_matrix, preferred_element_typ...]
    reshape x2 -> x0, local copies, waits for them, and re-layouts: 18.9 us -> none  [the longest x1 11.3 us: per_device(): flat_spectra = spectra.reshape(keep_count, 2, frames * input_width)]
  transfers between devices with their start and end apart: 4 -> 4, of which waited for: 2 -> 2; matrix products, arithmetic and copies ran while one was open for 4% -> 2% of each run, Pallas kernels for 0% -> 0%
where the time goes in v1:
time: 1050 us; the launch traced here: 1030 us
  waiting for transfers between devices  436 us (42%)
  local copies, waits for them, and re-layouts  403 us (38%)
  starting transfers between devices  94.2 us (9%)
  other arithmetic  61.1 us (6%)
  matrix products  32.4 us (3%)
    ppermute x3, waiting for transfers between devices, passed_along(): lax.ppermute(value, axis, [(source, source + steps) for source in range(f...  382 us
    another operation x129, local copies, waits for them, and re-layouts, per_device(): jnp.stack(jnp.split(flat_spectra, lax.axis_size(('tm', 'inp')), axis=0))  109 us
    unnamed x255, local copies, waits for them, and re-layouts  107 us
    all_to_all x1, starting transfers between devices, per_device(): lax.all_to_all(jnp.stack(jnp.split(flat_spectra, lax.axis_size(('tm', 'in...  80.1 us
    split x135, local copies, waits for them, and re-layouts, per_device(): jnp.split(flat_spectra, lax.axis_size(('tm', 'inp')), axis=0)  75.7 us
    mul x2, local copies, waits for them, and re-layouts, finish(): products.reshape(chan_count, 2, all_inputs, all_inputs) * (1.0 / spec_total)  68.9 us
    all_to_all x1, waiting for transfers between devices, per_device(): lax.all_to_all(jnp.stack(jnp.split(flat_spectra, lax.axis_size(('tm', 'in...  53.5 us
    dot_general x1, other arithmetic, per_device(): jnp.einsum('rfna,rnsj->jsfa', filtered, dft_matrix, preferred_element_typ...  37.1 us
  transfers between devices with their start and end apart: 4, of which 2 were waited for; matrix products, arithmetic and copies ran while one was open for 2% of the time, Pallas kernels for 0%

profile of v1, /device:TPU:1, one launch (start us, length us, event | category | flops | bytes accessed | tf_op | source)
XLA Modules:
  0.0 1026.8 jit_solution(16448535983829707335)
XLA Ops:
  0.0 7.3 copy.11
  7.3 7.4 collective-permute-start.1
  14.7 1.9 collective-permute-start
  16.6 3.6 slice.257
  20.2 4.8 collective-permute-start.2
  25.0 9.2 negate_convert_fusion
  34.6 382.1 %collective-permute-done.2 = bf16[2,3,1024,512]{3,2,0,1:T(8,128)(2,1)} collective-permute-done((bf16[2,3,1024,512]{3,2,0,1:T(8,128)(2,1)S(1)}, bf16[2,3,1024,512]{3,2,0,1:T(8,128)(2,1)}, u32[]{:S(2)}, u32[]{:S(2)}) %collective-permute-start.2) | collective-permute-done | bytes 6291488 | tf_op jit(solution)/shard_map/ppermute | solution.py:13
  416.7 3.6 constant_dynamic-update-slice_fusion.5
  420.3 7.5 constant_dynamic-update-slice_fusion.3
  427.8 12.4 %constant_dynamic-update-slice_fusion.1 = (bf16[2,8,1024,512]{3,2,0,1:T(8,128)(2,1)}, bf16[2,8,1024,512]{3,2,0,1:T(8,128)(2,1)}) fusion(bf16[2,4,1024,512]{3,2,0,1:T(8,128)(2,1)} %collective-permute-done, bf16[2,8,1024,512]{3,2,0,1:T(8,128)(2,1)} %get-tuple-element.7), kind=kLoop, calls=%fused_computation.37 | loop fusion | bytes 25165824
  440.9 7.2 constant_dynamic-update-slice_fusion
  448.0 37.1 %fusion.36 = bf16[2,4,1024,512,1]{3,2,0,1,4:T(8,128)(2,1)} fusion(bf16[2,7,1024,512]{3,2,0,1:T(8,128)(2,1)} %copy-done, f32[1024]{0:T(1024)S(1)} %bitcast.88, f32[1024]{0:T(1024)S(1)} %bitcast.89, f32[1024]{0:T(1024)S(1)} %bitcast.90, bf16[2,4,1024,512]{3,2,0,1:T(8,128)(2,1)} %collective-permute-done.1, f32[1024]{0:T(1024)S(1)} %bitcast.91, ...), kind=kLoop, calls=%fused_computation.12.clone.clone.clone.2 | loop fusion | flops 155189248 | bytes 109101056 | tf_op jit(solution)/shard_map/rfna,rnsj->jsfa/dot_general | solution.py:67
  485.2 11.7 %fusion.7 = bf16[512,2,4,512]{3,0,2,1:T(8,128)(2,1)S(1)} fusion(bf16[1,1024,2,512]{1,3,0,2:T(8,128)(2,1)S(1)} %get-tuple-element.140, bf16[1,1024,2,512]{1,3,0,2:T(8,128)(2,1)S(1)} %get-tuple-element.139, bf16[2,4,1024,512,1]{3,2,0,1,4:T(8,128)(2,1)} %fusion.36), kind=kOutput, calls=%fused_computation.13 | convolution fusion | flops 8600420352 | bytes 16777216 | tf_op jit(solution)/shard_map/rfna,rnsj->jsfa/dot_general | solution.py:67
  501.0 1.4 stack.426
  502.4 1.4 constant_dynamic-update-slice_fusion.133
  503.8 1.4 copy.17
  506.5 1.4 copy.18
  507.9 1.4 stack.428
  509.3 1.4 copy.19
  510.7 1.4 stack.429
  512.0 1.4 copy.20
  513.4 1.4 stack.430
  514.8 1.4 copy.21
  517.5 1.4 copy.22
  518.9 1.4 stack.432
  520.3 1.4 copy.23
  523.1 1.4 copy.24
  524.4 1.4 stack.434
  525.8 1.4 copy.25
  528.6 1.4 copy.26
  531.3 1.4 copy.27
  532.7 1.4 stack.437
  534.1 1.4 copy.28
  535.4 1.4 stack.438
  536.8 1.4 copy.29
  538.2 1.4 stack.439
  539.6 1.4 copy.30
  540.9 1.4 stack.440
  542.3 1.4 copy.31
  543.7 1.4 stack.441
  545.1 1.4 copy.32
  546.4 1.4 stack.442
  547.8 1.4 copy.33
  550.6 1.4 copy.34
  551.9 1.4 stack.444
  553.3 1.4 copy.35
  554.7 1.4 stack.445
  605.5 1.4 stack.481
  630.2 1.4 stack.508
  643.2 1.4 stack.526
  649.4 1.4 stack.530
  651.4 1.4 stack.531
  764.7 80.1 %all-to-all-start = ((bf16[128,4,2,2048]{3,2,1,0:T(2,128)(2,1)}), bf16[128,4,2,2048]{3,2,1,0:T(2,128)(2,1)}, u32[]{:S(2)}, u32[]{:S(2)}) async-start(bf16[128,4,2,2048]{3,2,1,0:T(2,128)(2,1)} %constant_dynamic-update-slice_fusion.6), calls=%async_computation | async-start | bytes 8388608 | tf_op jit(solution)/shard_map/all_to_all | solution.py:72
  845.1 53.5 %all-to-all-done = bf16[128,4,2,2048]{3,2,1,0:T(2,128)(2,1)} async-done(((bf16[128,4,2,2048]{3,2,1,0:T(2,128)(2,1)}), bf16[128,4,2,2048]{3,2,1,0:T(2,128)(2,1)}, u32[]{:S(2)}, u32[]{:S(2)}) %all-to-all-start) | async-done | bytes 4194336 | tf_op jit(solution)/shard_map/all_to_all | solution.py:72
  898.5 7.6 reshape.427
  906.1 7.6 reshape.426
  913.8 3.6 fusion.24
  918.5 2.4 copy_negate_fusion
  921.0 4.4 copy.148
  925.4 2.4 maximum_bitcast_fusion.4
  927.8 20.7 %fusion = bf16[4,2,2,512,2,512]{3,5,2,4,1,0:T(8,128)(2,1)} fusion(bf16[4,1,2,64,2,4,512]{6,3,2,5,4,1,0:T(8,128)(2,1)} %maximum_bitcast_fusion.4, bf16[4,1,2,64,2,4,512]{6,3,2,5,4,1,0:T(8,128)(2,1)} %copy.148, bf16[4,2,64,2,4,512,1,1]{5,4,1,0,3,2,7,6:T(4,128)(2,1)} %bitcast.86), kind=kOutput, calls=%fused_computation.1 | convolution fusion | flops 8623489024 | bytes 29360128 | tf_op jit(solution)/shard_map/crtgfa,csrthfb->csgahb/dot_general | solution.py:84
  948.4 41.4 %copy.150 = bf16[4,2,2,512,2,512]{5,4,3,2,1,0:T(2,128)(2,1)} copy(bf16[4,2,2,512,2,512]{3,5,2,4,1,0:T(8,128)(2,1)} %fusion) | data formatting | bytes 33554432 | tf_op jit(solution)/shard_map/mul | solution.py:31
  989.8 27.4 %mul.287 = bf16[4,2,1024,1024]{3,2,1,0:T(8,128)(2,1)} reshape(bf16[4,2,2,512,2,512]{5,4,3,2,1,0:T(2,128)(2,1)} %copy.150) | data formatting | bytes 33554432 | tf_op jit(solution)/shard_map/mul | solution.py:31
  1017.3 9.3 fusion.2
  (484 shorter events, 216.1 us)
Async XLA Ops:
  7.3 17.7 %copy-start.61 = (s32[12,1024]{1,0:T(8,128)S(1)}, s32[12,1024]{1,0:T(8,128)}, u32[]{:S(2)}) copy-start(s32[12,1024]{1,0:T(8,128)} %param.3) | copy-start | bytes 147460
  7.3 412.9 %collective-permute-start.1 = (bf16[2,4,1024,512]{3,2,0,1:T(8,128)(2,1)}, bf16[2,4,1024,512]{3,2,0,1:T(8,128)(2,1)}, u32[]{:S(2)}, u32[]{:S(2)}) collective-permute-start(bf16[2,4,1024,512]{3,2,0,1:T(8,128)(2,1)} %copy.11), channel_id=1, source_target_pairs={{0,4},{2,6},{4,8},{6,10},{8,12},{10,14},{12,16},{14,18},{16,20},{1... | collective-permute-start | bytes 25165832 | tf_op jit(solution)/shard_map/ppermute | solution.py:13
  14.7 413.1 %collective-permute-start = (bf16[2,4,1024,512]{3,2,0,1:T(8,128)(2,1)}, bf16[2,4,1024,512]{3,2,0,1:T(8,128)(2,1)}, u32[]{:S(2)}, u32[]{:S(2)}) collective-permute-start(bf16[2,4,1024,512]{3,2,0,1:T(8,128)(2,1)} %copy.11), channel_id=1, source_target_pairs={{0,2},{2,4},{4,6},{6,8},{8,10},{10,12},{12,14},{14,16},{16,18},{18... | collective-permute-start | bytes 25165832 | tf_op jit(solution)/shard_map/ppermute | solution.py:13
  20.2 396.5 %collective-permute-start.2 = (bf16[2,3,1024,512]{3,2,0,1:T(8,128)(2,1)S(1)}, bf16[2,3,1024,512]{3,2,0,1:T(8,128)(2,1)}, u32[]{:S(2)}, u32[]{:S(2)}) collective-permute-start(bf16[2,3,1024,512]{3,2,0,1:T(8,128)(2,1)S(1)} %slice.257), channel_id=1, source_target_pairs={{0,6},{2,8},{4,10},{6,12},{8,14},{10,16},{12,18},{14,20},{16,22},{... | collective-permute-start | bytes 18874376 | tf_op jit(solution)/shard_map/ppermute | solution.py:13
  612.6 70.7 %copy-start.2 = (bf16[1,4,2,2048]{3,2,1,0:T(2,128)(2,1)S(1)}, bf16[1,4,2,2048]{3,2,1,0:T(2,128)(2,1)}, u32[]{:S(2)}) copy-start(bf16[1,4,2,2048]{3,2,1,0:T(2,128)(2,1)} %stack.427) | copy-start | bytes 98308
  612.7 71.4 %copy-start.3 = (bf16[1,4,2,2048]{3,2,1,0:T(2,128)(2,1)S(1)}, bf16[1,4,2,2048]{3,2,1,0:T(2,128)(2,1)}, u32[]{:S(2)}) copy-start(bf16[1,4,2,2048]{3,2,1,0:T(2,128)(2,1)} %stack.428) | copy-start | bytes 98308
  613.3 71.4 %copy-start.4 = (bf16[1,4,2,2048]{3,2,1,0:T(2,128)(2,1)S(1)}, bf16[1,4,2,2048]{3,2,1,0:T(2,128)(2,1)}, u32[]{:S(2)}) copy-start(bf16[1,4,2,2048]{3,2,1,0:T(2,128)(2,1)} %stack.429) | copy-start | bytes 98308
  613.3 72.0 %copy-start.5 = (bf16[1,4,2,2048]{3,2,1,0:T(2,128)(2,1)S(1)}, bf16[1,4,2,2048]{3,2,1,0:T(2,128)(2,1)}, u32[]{:S(2)}) copy-start(bf16[1,4,2,2048]{3,2,1,0:T(2,128)(2,1)} %stack.430) | copy-start | bytes 98308
  613.9 72.0 %copy-start.6 = (bf16[1,4,2,2048]{3,2,1,0:T(2,128)(2,1)S(1)}, bf16[1,4,2,2048]{3,2,1,0:T(2,128)(2,1)}, u32[]{:S(2)}) copy-start(bf16[1,4,2,2048]{3,2,1,0:T(2,128)(2,1)} %stack.431) | copy-start | bytes 98308
  614.0 72.6 %copy-start.7 = (bf16[1,4,2,2048]{3,2,1,0:T(2,128)(2,1)S(1)}, bf16[1,4,2,2048]{3,2,1,0:T(2,128)(2,1)}, u32[]{:S(2)}) copy-start(bf16[1,4,2,2048]{3,2,1,0:T(2,128)(2,1)} %stack.432) | copy-start | bytes 98308
  614.6 72.6 %copy-start.8 = (bf16[1,4,2,2048]{3,2,1,0:T(2,128)(2,1)S(1)}, bf16[1,4,2,2048]{3,2,1,0:T(2,128)(2,1)}, u32[]{:S(2)}) copy-start(bf16[1,4,2,2048]{3,2,1,0:T(2,128)(2,1)} %stack.433) | copy-start | bytes 98308
  614.6 73.3 %copy-start.9 = (bf16[1,4,2,2048]{3,2,1,0:T(2,128)(2,1)S(1)}, bf16[1,4,2,2048]{3,2,1,0:T(2,128)(2,1)}, u32[]{:S(2)}) copy-start(bf16[1,4,2,2048]{3,2,1,0:T(2,128)(2,1)} %stack.434) | copy-start | bytes 98308
  615.2 73.3 %copy-start.10 = (bf16[1,4,2,2048]{3,2,1,0:T(2,128)(2,1)S(1)}, bf16[1,4,2,2048]{3,2,1,0:T(2,128)(2,1)}, u32[]{:S(2)}) copy-start(bf16[1,4,2,2048]{3,2,1,0:T(2,128)(2,1)} %stack.435) | copy-start | bytes 98308
  615.3 73.9 %copy-start.11 = (bf16[1,4,2,2048]{3,2,1,0:T(2,128)(2,1)S(1)}, bf16[1,4,2,2048]{3,2,1,0:T(2,128)(2,1)}, u32[]{:S(2)}) copy-start(bf16[1,4,2,2048]{3,2,1,0:T(2,128)(2,1)} %stack.436) | copy-start | bytes 98308
  615.9 73.9 %copy-start.12 = (bf16[1,4,2,2048]{3,2,1,0:T(2,128)(2,1)S(1)}, bf16[1,4,2,2048]{3,2,1,0:T(2,128)(2,1)}, u32[]{:S(2)}) copy-start(bf16[1,4,2,2048]{3,2,1,0:T(2,128)(2,1)} %stack.437) | copy-start | bytes 98308
  615.9 74.5 %copy-start.13 = (bf16[1,4,2,2048]{3,2,1,0:T(2,128)(2,1)S(1)}, bf16[1,4,2,2048]{3,2,1,0:T(2,128)(2,1)}, u32[]{:S(2)}) copy-start(bf16[1,4,2,2048]{3,2,1,0:T(2,128)(2,1)} %stack.438) | copy-start | bytes 98308
  616.5 74.5 %copy-start.14 = (bf16[1,4,2,2048]{3,2,1,0:T(2,128)(2,1)S(1)}, bf16[1,4,2,2048]{3,2,1,0:T(2,128)(2,1)}, u32[]{:S(2)}) copy-start(bf16[1,4,2,2048]{3,2,1,0:T(2,128)(2,1)} %stack.439) | copy-start | bytes 98308
  616.6 75.2 %copy-start.15 = (bf16[1,4,2,2048]{3,2,1,0:T(2,128)(2,1)S(1)}, bf16[1,4,2,2048]{3,2,1,0:T(2,128)(2,1)}, u32[]{:S(2)}) copy-start(bf16[1,4,2,2048]{3,2,1,0:T(2,128)(2,1)} %stack.440) | copy-start | bytes 98308
  617.2 75.2 %copy-start.16 = (bf16[1,4,2,2048]{3,2,1,0:T(2,128)(2,1)S(1)}, bf16[1,4,2,2048]{3,2,1,0:T(2,128)(2,1)}, u32[]{:S(2)}) copy-start(bf16[1,4,2,2048]{3,2,1,0:T(2,128)(2,1)} %stack.441) | copy-start | bytes 98308
  617.2 75.8 %copy-start.17 = (bf16[1,4,2,2048]{3,2,1,0:T(2,128)(2,1)S(1)}, bf16[1,4,2,2048]{3,2,1,0:T(2,128)(2,1)}, u32[]{:S(2)}) copy-start(bf16[1,4,2,2048]{3,2,1,0:T(2,128)(2,1)} %stack.442) | copy-start | bytes 98308
  617.8 75.8 %copy-start.18 = (bf16[1,4,2,2048]{3,2,1,0:T(2,128)(2,1)S(1)}, bf16[1,4,2,2048]{3,2,1,0:T(2,128)(2,1)}, u32[]{:S(2)}) copy-start(bf16[1,4,2,2048]{3,2,1,0:T(2,128)(2,1)} %stack.443) | copy-start | bytes 98308
  617.9 76.4 %copy-start.19 = (bf16[1,4,2,2048]{3,2,1,0:T(2,128)(2,1)S(1)}, bf16[1,4,2,2048]{3,2,1,0:T(2,128)(2,1)}, u32[]{:S(2)}) copy-start(bf16[1,4,2,2048]{3,2,1,0:T(2,128)(2,1)} %stack.444) | copy-start | bytes 98308
  618.5 76.5 %copy-start.20 = (bf16[1,4,2,2048]{3,2,1,0:T(2,128)(2,1)S(1)}, bf16[1,4,2,2048]{3,2,1,0:T(2,128)(2,1)}, u32[]{:S(2)}) copy-start(bf16[1,4,2,2048]{3,2,1,0:T(2,128)(2,1)} %stack.445) | copy-start | bytes 98308
  636.7 81.2 %copy-start.21 = (bf16[1,4,2,2048]{3,2,1,0:T(2,128)(2,1)S(1)}, bf16[1,4,2,2048]{3,2,1,0:T(2,128)(2,1)}, u32[]{:S(2)}) copy-start(bf16[1,4,2,2048]{3,2,1,0:T(2,128)(2,1)} %stack.481) | copy-start | bytes 98308
  637.4 81.2 %copy-start.22 = (bf16[1,4,2,2048]{3,2,1,0:T(2,128)(2,1)S(1)}, bf16[1,4,2,2048]{3,2,1,0:T(2,128)(2,1)}, u32[]{:S(2)}) copy-start(bf16[1,4,2,2048]{3,2,1,0:T(2,128)(2,1)} %stack.482) | copy-start | bytes 98308
  637.4 81.8 %copy-start.23 = (bf16[1,4,2,2048]{3,2,1,0:T(2,128)(2,1)S(1)}, bf16[1,4,2,2048]{3,2,1,0:T(2,128)(2,1)}, u32[]{:S(2)}) copy-start(bf16[1,4,2,2048]{3,2,1,0:T(2,128)(2,1)} %stack.483) | copy-start | bytes 98308
  638.0 81.8 %copy-start.24 = (bf16[1,4,2,2048]{3,2,1,0:T(2,128)(2,1)S(1)}, bf16[1,4,2,2048]{3,2,1,0:T(2,128)(2,1)}, u32[]{:S(2)}) copy-start(bf16[1,4,2,2048]{3,2,1,0:T(2,128)(2,1)} %stack.484) | copy-start | bytes 98308
  638.0 82.5 %copy-start.25 = (bf16[1,4,2,2048]{3,2,1,0:T(2,128)(2,1)S(1)}, bf16[1,4,2,2048]{3,2,1,0:T(2,128)(2,1)}, u32[]{:S(2)}) copy-start(bf16[1,4,2,2048]{3,2,1,0:T(2,128)(2,1)} %stack.485) | copy-start | bytes 98308
  638.7 82.5 %copy-start.26 = (bf16[1,4,2,2048]{3,2,1,0:T(2,128)(2,1)S(1)}, bf16[1,4,2,2048]{3,2,1,0:T(2,128)(2,1)}, u32[]{:S(2)}) copy-start(bf16[1,4,2,2048]{3,2,1,0:T(2,128)(2,1)} %stack.486) | copy-start | bytes 98308
  638.7 83.1 %copy-start.27 = (bf16[1,4,2,2048]{3,2,1,0:T(2,128)(2,1)S(1)}, bf16[1,4,2,2048]{3,2,1,0:T(2,128)(2,1)}, u32[]{:S(2)}) copy-start(bf16[1,4,2,2048]{3,2,1,0:T(2,128)(2,1)} %stack.487) | copy-start | bytes 98308
  639.3 83.1 %copy-start.28 = (bf16[1,4,2,2048]{3,2,1,0:T(2,128)(2,1)S(1)}, bf16[1,4,2,2048]{3,2,1,0:T(2,128)(2,1)}, u32[]{:S(2)}) copy-start(bf16[1,4,2,2048]{3,2,1,0:T(2,128)(2,1)} %stack.488) | copy-start | bytes 98308
  639.3 83.7 %copy-start.29 = (bf16[1,4,2,2048]{3,2,1,0:T(2,128)(2,1)S(1)}, bf16[1,4,2,2048]{3,2,1,0:T(2,128)(2,1)}, u32[]{:S(2)}) copy-start(bf16[1,4,2,2048]{3,2,1,0:T(2,128)(2,1)} %stack.489) | copy-start | bytes 98308
  640.0 83.7 %copy-start.30 = (bf16[1,4,2,2048]{3,2,1,0:T(2,128)(2,1)S(1)}, bf16[1,4,2,2048]{3,2,1,0:T(2,128)(2,1)}, u32[]{:S(2)}) copy-start(bf16[1,4,2,2048]{3,2,1,0:T(2,128)(2,1)} %stack.490) | copy-start | bytes 98308
  640.0 84.4 %copy-start.31 = (bf16[1,4,2,2048]{3,2,1,0:T(2,128)(2,1)S(1)}, bf16[1,4,2,2048]{3,2,1,0:T(2,128)(2,1)}, u32[]{:S(2)}) copy-start(bf16[1,4,2,2048]{3,2,1,0:T(2,128)(2,1)} %stack.491) | copy-start | bytes 98308
  640.6 84.4 %copy-start.32 = (bf16[1,4,2,2048]{3,2,1,0:T(2,128)(2,1)S(1)}, bf16[1,4,2,2048]{3,2,1,0:T(2,128)(2,1)}, u32[]{:S(2)}) copy-start(bf16[1,4,2,2048]{3,2,1,0:T(2,128)(2,1)} %stack.492) | copy-start | bytes 98308
  640.6 85.0 %copy-start.33 = (bf16[1,4,2,2048]{3,2,1,0:T(2,128)(2,1)S(1)}, bf16[1,4,2,2048]{3,2,1,0:T(2,128)(2,1)}, u32[]{:S(2)}) copy-start(bf16[1,4,2,2048]{3,2,1,0:T(2,128)(2,1)} %stack.493) | copy-start | bytes 98308
  641.3 85.0 %copy-start.34 = (bf16[1,4,2,2048]{3,2,1,0:T(2,128)(2,1)S(1)}, bf16[1,4,2,2048]{3,2,1,0:T(2,128)(2,1)}, u32[]{:S(2)}) copy-start(bf16[1,4,2,2048]{3,2,1,0:T(2,128)(2,1)} %stack.494) | copy-start | bytes 98308
  641.3 85.6 %copy-start.35 = (bf16[1,4,2,2048]{3,2,1,0:T(2,128)(2,1)S(1)}, bf16[1,4,2,2048]{3,2,1,0:T(2,128)(2,1)}, u32[]{:S(2)}) copy-start(bf16[1,4,2,2048]{3,2,1,0:T(2,128)(2,1)} %stack.495) | copy-start | bytes 98308
  641.9 85.6 %copy-start.36 = (bf16[1,4,2,2048]{3,2,1,0:T(2,128)(2,1)S(1)}, bf16[1,4,2,2048]{3,2,1,0:T(2,128)(2,1)}, u32[]{:S(2)}) copy-start(bf16[1,4,2,2048]{3,2,1,0:T(2,128)(2,1)} %stack.496) | copy-start | bytes 98308
  641.9 86.3 %copy-start.37 = (bf16[1,4,2,2048]{3,2,1,0:T(2,128)(2,1)S(1)}, bf16[1,4,2,2048]{3,2,1,0:T(2,128)(2,1)}, u32[]{:S(2)}) copy-start(bf16[1,4,2,2048]{3,2,1,0:T(2,128)(2,1)} %stack.497) | copy-start | bytes 98308
  642.6 86.3 %copy-start.38 = (bf16[1,4,2,2048]{3,2,1,0:T(2,128)(2,1)S(1)}, bf16[1,4,2,2048]{3,2,1,0:T(2,128)(2,1)}, u32[]{:S(2)}) copy-start(bf16[1,4,2,2048]{3,2,1,0:T(2,128)(2,1)} %stack.498) | copy-start | bytes 98308
  643.2 86.3 %copy-start.39 = (bf16[1,4,2,2048]{3,2,1,0:T(2,128)(2,1)S(1)}, bf16[1,4,2,2048]{3,2,1,0:T(2,128)(2,1)}, u32[]{:S(2)}) copy-start(bf16[1,4,2,2048]{3,2,1,0:T(2,128)(2,1)} %stack.499) | copy-start | bytes 98308
  650.8 84.5 %copy-start.40 = (bf16[1,4,2,2048]{3,2,1,0:T(2,128)(2,1)S(1)}, bf16[1,4,2,2048]{3,2,1,0:T(2,128)(2,1)}, u32[]{:S(2)}) copy-start(bf16[1,4,2,2048]{3,2,1,0:T(2,128)(2,1)} %stack.508) | copy-start | bytes 98308
  651.4 84.5 %copy-start.41 = (bf16[1,4,2,2048]{3,2,1,0:T(2,128)(2,1)S(1)}, bf16[1,4,2,2048]{3,2,1,0:T(2,128)(2,1)}, u32[]{:S(2)}) copy-start(bf16[1,4,2,2048]{3,2,1,0:T(2,128)(2,1)} %stack.509) | copy-start | bytes 98308
  684.6 51.9 %copy-start.42 = (bf16[1,4,2,2048]{3,2,1,0:T(2,128)(2,1)S(1)}, bf16[1,4,2,2048]{3,2,1,0:T(2,128)(2,1)}, u32[]{:S(2)}) copy-start(bf16[1,4,2,2048]{3,2,1,0:T(2,128)(2,1)} %stack.510) | copy-start | bytes 98308
  685.3 51.9 %copy-start.43 = (bf16[1,4,2,2048]{3,2,1,0:T(2,128)(2,1)S(1)}, bf16[1,4,2,2048]{3,2,1,0:T(2,128)(2,1)}, u32[]{:S(2)}) copy-start(bf16[1,4,2,2048]{3,2,1,0:T(2,128)(2,1)} %stack.511) | copy-start | bytes 98308
  685.9 51.9 %copy-start.44 = (bf16[1,4,2,2048]{3,2,1,0:T(2,128)(2,1)S(1)}, bf16[1,4,2,2048]{3,2,1,0:T(2,128)(2,1)}, u32[]{:S(2)}) copy-start(bf16[1,4,2,2048]{3,2,1,0:T(2,128)(2,1)} %stack.512) | copy-start | bytes 98308
  686.6 51.9 %copy-start.45 = (bf16[1,4,2,2048]{3,2,1,0:T(2,128)(2,1)S(1)}, bf16[1,4,2,2048]{3,2,1,0:T(2,128)(2,1)}, u32[]{:S(2)}) copy-start(bf16[1,4,2,2048]{3,2,1,0:T(2,128)(2,1)} %stack.513) | copy-start | bytes 98308
  687.2 51.9 %copy-start.46 = (bf16[1,4,2,2048]{3,2,1,0:T(2,128)(2,1)S(1)}, bf16[1,4,2,2048]{3,2,1,0:T(2,128)(2,1)}, u32[]{:S(2)}) copy-start(bf16[1,4,2,2048]{3,2,1,0:T(2,128)(2,1)} %stack.514) | copy-start | bytes 98308
  687.9 51.9 %copy-start.47 = (bf16[1,4,2,2048]{3,2,1,0:T(2,128)(2,1)S(1)}, bf16[1,4,2,2048]{3,2,1,0:T(2,128)(2,1)}, u32[]{:S(2)}) copy-start(bf16[1,4,2,2048]{3,2,1,0:T(2,128)(2,1)} %stack.515) | copy-start | bytes 98308
  688.5 51.9 %copy-start.48 = (bf16[1,4,2,2048]{3,2,1,0:T(2,128)(2,1)S(1)}, bf16[1,4,2,2048]{3,2,1,0:T(2,128)(2,1)}, u32[]{:S(2)}) copy-start(bf16[1,4,2,2048]{3,2,1,0:T(2,128)(2,1)} %stack.516) | copy-start | bytes 98308
  689.2 51.9 %copy-start.49 = (bf16[1,4,2,2048]{3,2,1,0:T(2,128)(2,1)S(1)}, bf16[1,4,2,2048]{3,2,1,0:T(2,128)(2,1)}, u32[]{:S(2)}) copy-start(bf16[1,4,2,2048]{3,2,1,0:T(2,128)(2,1)} %stack.517) | copy-start | bytes 98308
  689.8 51.9 %copy-start.50 = (bf16[1,4,2,2048]{3,2,1,0:T(2,128)(2,1)S(1)}, bf16[1,4,2,2048]{3,2,1,0:T(2,128)(2,1)}, u32[]{:S(2)}) copy-start(bf16[1,4,2,2048]{3,2,1,0:T(2,128)(2,1)} %stack.518) | copy-start | bytes 98308
  690.4 51.9 %copy-start.51 = (bf16[1,4,2,2048]{3,2,1,0:T(2,128)(2,1)S(1)}, bf16[1,4,2,2048]{3,2,1,0:T(2,128)(2,1)}, u32[]{:S(2)}) copy-start(bf16[1,4,2,2048]{3,2,1,0:T(2,128)(2,1)} %stack.519) | copy-start | bytes 98308
  691.1 51.9 %copy-start.52 = (bf16[1,4,2,2048]{3,2,1,0:T(2,128)(2,1)S(1)}, bf16[1,4,2,2048]{3,2,1,0:T(2,128)(2,1)}, u32[]{:S(2)}) copy-start(bf16[1,4,2,2048]{3,2,1,0:T(2,128)(2,1)} %stack.520) | copy-start | bytes 98308
  691.7 51.8 %copy-start.53 = (bf16[1,4,2,2048]{3,2,1,0:T(2,128)(2,1)S(1)}, bf16[1,4,2,2048]{3,2,1,0:T(2,128)(2,1)}, u32[]{:S(2)}) copy-start(bf16[1,4,2,2048]{3,2,1,0:T(2,128)(2,1)} %stack.521) | copy-start | bytes 98308
  692.4 51.8 %copy-start.54 = (bf16[1,4,2,2048]{3,2,1,0:T(2,128)(2,1)S(1)}, bf16[1,4,2,2048]{3,2,1,0:T(2,128)(2,1)}, u32[]{:S(2)}) copy-start(bf16[1,4,2,2048]{3,2,1,0:T(2,128)(2,1)} %stack.522) | copy-start | bytes 98308
  693.0 51.8 %copy-start.55 = (bf16[1,4,2,2048]{3,2,1,0:T(2,128)(2,1)S(1)}, bf16[1,4,2,2048]{3,2,1,0:T(2,128)(2,1)}, u32[]{:S(2)}) copy-start(bf16[1,4,2,2048]{3,2,1,0:T(2,128)(2,1)} %stack.523) | copy-start | bytes 98308
  693.7 51.8 %copy-start.56 = (bf16[1,4,2,2048]{3,2,1,0:T(2,128)(2,1)S(1)}, bf16[1,4,2,2048]{3,2,1,0:T(2,128)(2,1)}, u32[]{:S(2)}) copy-start(bf16[1,4,2,2048]{3,2,1,0:T(2,128)(2,1)} %stack.524) | copy-start | bytes 98308
  694.3 51.8 %copy-start.57 = (bf16[1,4,2,2048]{3,2,1,0:T(2,128)(2,1)S(1)}, bf16[1,4,2,2048]{3,2,1,0:T(2,128)(2,1)}, u32[]{:S(2)}) copy-start(bf16[1,4,2,2048]{3,2,1,0:T(2,128)(2,1)} %stack.525) | copy-start | bytes 98308
  694.9 51.8 %copy-start.58 = (bf16[1,4,2,2048]{3,2,1,0:T(2,128)(2,1)S(1)}, bf16[1,4,2,2048]{3,2,1,0:T(2,128)(2,1)}, u32[]{:S(2)}) copy-start(bf16[1,4,2,2048]{3,2,1,0:T(2,128)(2,1)} %stack.526) | copy-start | bytes 98308
  695.6 53.8 %copy-start.59 = (bf16[1,4,2,2048]{3,2,1,0:T(2,128)(2,1)S(1)}, bf16[1,4,2,2048]{3,2,1,0:T(2,128)(2,1)}, u32[]{:S(2)}) copy-start(bf16[1,4,2,2048]{3,2,1,0:T(2,128)(2,1)} %stack.530) | copy-start | bytes 98308
  696.2 53.8 %copy-start.60 = (bf16[1,4,2,2048]{3,2,1,0:T(2,128)(2,1)S(1)}, bf16[1,4,2,2048]{3,2,1,0:T(2,128)(2,1)}, u32[]{:S(2)}) copy-start(bf16[1,4,2,2048]{3,2,1,0:T(2,128)(2,1)} %stack.531) | copy-start | bytes 98308
  764.7 133.9 %all-to-all-start = ((bf16[128,4,2,2048]{3,2,1,0:T(2,128)(2,1)}), bf16[128,4,2,2048]{3,2,1,0:T(2,128)(2,1)}, u32[]{:S(2)}, u32[]{:S(2)}) async-start(bf16[128,4,2,2048]{3,2,1,0:T(2,128)(2,1)} %constant_dynamic-update-slice_fusion.6), calls=%async_computation | async-start | bytes 8388608 | tf_op jit(solution)/shard_map/all_to_all | solution.py:72
  (2 other events, 16.7 us)
